TPU v7x, 32 devices: a whole 2x2x4 slice. The times are simulated.
32 devices in a mesh: seq: 4 (over y, x), head: 8 (over z, core).
Axes of the slice: x: 2, y: 2, z: 4, core: 2. Of those that a mesh axis runs over, the one named last changes fastest.
Arguments:
- sequence_activity: bfloat16 [2, 2048, 4096], P(None, 'seq', 'head'), may hold values from -6 to 6
- lookup_mapping_tensor: bfloat16 [4096, 8, 768], P(None, 'head'), may hold values from -1 to 1, as said below
- stepsize_mapping_matrix: bfloat16 [4096, 8], P(None, 'head'), may hold values from -0.09375 to 0.09375
- logit_sharpness: float32 [8], P('head'), may hold values from 4 to 120
- adapter_gain_vector: float32 [8, 256], P('head'), may hold values from 0.1 to 1.9
- starting_inner_left_matrix: float32 [8, 256, 512], P('head'), may hold values from -0.375 to 0.375
- starting_inner_right_matrix: float32 [8, 512, 256], P('head'), may hold values from -0.25 to 0.25
- final_mixing_matrix: bfloat16 [8, 256, 4096], P('head'), may hold values from -0.125 to 0.125
Outputs:
- mixed: bfloat16 [2, 2048, 4096], P(None, 'seq', 'head')
Inputs may be any that keep to these rules, and one draw needn't show every extreme that they name: `lookup_mapping_tensor`: entries of order 1 / sqrt(4096).
All inputs are finite; a program needn't handle non-finite values.
Results may differ from a plain program's by a relative error of at most 0.02.
Values may be sent and summed in bfloat16 or wider, within the bound.
No kernel may reach another device: no remote copies, remote signals or barrier semaphores. Data moves between devices by JAX's collectives and lax.ppermute only.
A program may use at most 64 MiB of HBM per device.

v0:
```python
import jax
import jax.numpy as jnp
from jax import lax
from jax.sharding import PartitionSpec as P

WIN = 2048
NS_STEPS = 3
update_rate = 0.3


def shifted(block, axis, distance):
    devices = range(lax.axis_size(axis))
    route = [(i - distance, i) for i in devices if i - distance in devices]
    return lax.ppermute(block, axis, route)


def orthogonalize(update):
    scale = lax.rsqrt(jnp.sum(update * update) + 1e-06)
    current = update * scale
    for sweep in range(NS_STEPS):
        if current.shape[0] <= current.shape[1]:
            gram = jnp.dot(current, current.T, precision=lax.Precision.HIGHEST)
            current = 1.5 * current - 0.5 * jnp.dot(gram, current, precision=lax.Precision.HIGHEST)
        else:
            gram = jnp.dot(current.T, current, precision=lax.Precision.HIGHEST)
            current = 1.5 * current - 0.5 * jnp.dot(current, gram, precision=lax.Precision.HIGHEST)
    return current


def fast_group(weight_in, weight_out, keys, weighted, query_rows):
    in_half = weight_in.astype(jnp.bfloat16)
    out_half = weight_out.astype(jnp.bfloat16)
    hidden = jnp.dot(keys, in_half, preferred_element_type=jnp.float32)
    gating = jax.nn.sigmoid(hidden)
    activated = (hidden * gating).astype(jnp.bfloat16)
    grad_out = jnp.dot(activated.T, weighted, preferred_element_type=jnp.float32)
    backward = jnp.dot(weighted, out_half.T, preferred_element_type=jnp.float32)
    slopes = (backward * gating * (1.0 + hidden * (1.0 - gating))).astype(jnp.bfloat16)
    grad_in = jnp.dot(keys.T, slopes, preferred_element_type=jnp.float32)
    new_in = weight_in + update_rate * orthogonalize(grad_in)
    new_out = weight_out + update_rate * orthogonalize(grad_out)
    query_hidden = jnp.dot(
        query_rows, new_in.astype(jnp.bfloat16), preferred_element_type=jnp.float32
    )
    query_act = jax.nn.silu(query_hidden).astype(jnp.bfloat16)
    fast = jnp.dot(query_act, new_out.astype(jnp.bfloat16), preferred_element_type=jnp.float32)
    return (new_in, new_out, fast)


def prepare(projected, rate_col, count_seqs):
    head_dim = projected.shape[1] // 3
    query_rows = projected[:, :head_dim]
    keys = projected[:, head_dim : 2 * head_dim]
    values = projected[:, 2 * head_dim :]
    query_norm = (
        query_rows * lax.rsqrt(jnp.sum(query_rows * query_rows, axis=1, keepdims=True) + 1e-06)
    ).astype(jnp.bfloat16)
    key_norm = (keys * lax.rsqrt(jnp.sum(keys * keys, axis=1, keepdims=True) + 1e-06)).astype(
        jnp.bfloat16
    )
    value_half = values.astype(jnp.bfloat16)
    weighted = (jax.nn.softplus(rate_col) * values).astype(jnp.bfloat16)
    return (
        query_norm.reshape(count_seqs, -1, head_dim),
        key_norm.reshape(count_seqs, -1, head_dim),
        value_half.reshape(count_seqs, -1, head_dim),
        weighted.reshape(count_seqs, -1, head_dim),
    )


def attend_window(query_rows, keys, values, scale, start):
    count = query_rows.shape[1]
    window = keys.shape[1] - count
    scores = scale * jnp.einsum(
        "sqd,skd->sqk", query_rows, keys, preferred_element_type=jnp.float32
    )
    row_pos = lax.broadcasted_iota(jnp.int32, (count, count + window), 0)
    col_pos = lax.broadcasted_iota(jnp.int32, (count, count + window), 1)
    valid = (col_pos >= row_pos) & (col_pos <= row_pos + window) & (col_pos + start >= window)
    scores = jnp.where(valid[None], scores, -1e30)
    highest = jnp.max(scores, axis=2, keepdims=True)
    weights = jnp.exp(scores - highest)
    probs = (weights / jnp.sum(weights, axis=2, keepdims=True)).astype(jnp.bfloat16)
    return jnp.einsum("sqk,skd->sqd", probs, values, preferred_element_type=jnp.float32)


def combine(attended_output, fast, gain):
    normed = fast * lax.rsqrt(jnp.mean(fast * fast, axis=-1, keepdims=True) + 1e-05) * gain
    return (attended_output + normed).astype(jnp.bfloat16)


def body(
    sequence_activity,
    lookup_mapping_tensor,
    stepsize_mapping_matrix,
    logit_sharpness,
    adapter_gain_vector,
    starting_inner_left_matrix,
    starting_inner_right_matrix,
    final_mixing_matrix,
):
    seqs, head_group, local_width = sequence_activity.shape
    total_rows = seqs * head_group
    flattened = sequence_activity.reshape(total_rows, local_width)
    weights_in = lookup_mapping_tensor.reshape(
        lookup_mapping_tensor.shape[0], lookup_mapping_tensor.shape[2]
    )
    head_dim = weights_in.shape[1] // 3
    piece = lax.all_gather(flattened, "head", axis=1, tiled=True)
    projected = jnp.dot(piece, weights_in, preferred_element_type=jnp.float32)
    rate_col = jnp.dot(piece, stepsize_mapping_matrix, preferred_element_type=jnp.float32)
    query_rows, keys, values, weighted = prepare(projected, rate_col, seqs)
    token_position = lax.axis_index("seq")
    length = lax.axis_size("seq")
    reach = WIN // head_group
    hops = min(reach, length - 1)
    empty = jnp.zeros_like(keys)
    earlier = []
    current = (keys, values)
    for distance in range(hops):
        current = shifted((current[0], current[1]), "seq", 1)
        earlier.insert(0, current)
    for missing in range(reach - hops):
        earlier.insert(0, (empty, empty))
    windowed_key_rows = jnp.concatenate([pair[0] for pair in earlier] + [keys], axis=1)
    windowed_value_rows = jnp.concatenate([pair[1] for pair in earlier] + [values], axis=1)
    attended_output = attend_window(
        query_rows,
        windowed_key_rows,
        windowed_value_rows,
        logit_sharpness[0],
        token_position * head_group,
    )
    start_in = starting_inner_left_matrix[0]
    start_out = starting_inner_right_matrix[0]

    def turn(step, carry):
        held_in, held_out, fast_all = carry
        which = step // length
        live = step % length == token_position
        which = jnp.clip(which, 0, seqs - 1)
        use_in = jnp.where(token_position == 0, start_in, held_in)
        use_out = jnp.where(token_position == 0, start_out, held_out)
        block_keys = lax.dynamic_index_in_dim(keys, which, 0, keepdims=False)
        block_weighted = lax.dynamic_index_in_dim(weighted, which, 0, keepdims=False)
        block_queries = lax.dynamic_index_in_dim(query_rows, which, 0, keepdims=False)

        def working():
            return fast_group(use_in, use_out, block_keys, block_weighted, block_queries)

        def resting():
            return (use_in, use_out, jnp.zeros((head_group, head_dim), jnp.float32))

        new_in, new_out, fast = lax.cond(live, working, resting)
        stored = lax.dynamic_update_index_in_dim(fast_all, fast, which, 0)
        fast_all = jnp.where(live, stored, fast_all)
        sent_in, sent_out = shifted((new_in, new_out), "seq", 1)
        return (sent_in, sent_out, fast_all)

    turns = seqs * length
    carried = (start_in, start_out, jnp.zeros((seqs, head_group, head_dim), jnp.float32))
    carried = lax.fori_loop(0, turns, turn, carried)
    head_out = combine(attended_output, carried[2], adapter_gain_vector[0]).reshape(
        total_rows, head_dim
    )
    columns = lax.all_to_all(final_mixing_matrix, "head", split_axis=2, concat_axis=0, tiled=True)
    columns = columns.reshape(-1, columns.shape[2])
    result = jnp.dot(
        lax.all_gather(head_out, "head", axis=1, tiled=True),
        columns,
        preferred_element_type=jnp.float32,
    )
    return result.astype(jnp.bfloat16).reshape(seqs, head_group, -1)


def solution(mesh):
    in_specs = (
        P(None, "seq", "head"),
        P(None, "head", None),
        P(None, "head"),
        P("head"),
        P("head", None),
        P("head", None, None),
        P("head", None, None),
        P("head", None, None),
    )
    out_specs = P(None, "seq", "head")
    return jax.shard_map(body, mesh=mesh, in_specs=in_specs, out_specs=out_specs, check_vma=False)
```

profile of v0, /device:TPU:0, one launch (start us, length us, event | category | flops | bytes accessed | tf_op | source)
XLA Modules:
  0.0 614.8 jit_solution(14468545543711807388)
XLA Ops:
  7.3 86.4 %all-gather.3.cloned.1.call-done = bf16[1024,4096]{1,0:T(8,128)(2,1)} async-done(((bf16[1024,512]{1,0:T(8,128)(2,1)}), bf16[1024,4096]{1,0:T(8,128)(2,1)}) %all-gather.3.cloned.1.call-update) | async-done | bytes 8388624 | tf_op jit(solution)/shard_map/all_gather | solution.py:109
  93.7 5.8 fusion.86
  99.6 9.0 %fusion.61 = f32[1024,768]{1,0:T(8,128)S(1)} fusion(bf16[1024,4096]{1,0:T(8,128)(2,1)S(1)} %copy-done.3, bf16[4096,1,768]{2,0,1:T(8,128)(2,1)} %param.13), kind=kOutput, calls=%fused_computation.72 | convolution fusion | flops 6442450944 | bytes 17825792 | tf_op jit(solution)/shard_map/dot_general | solution.py:110
  110.7 3.4 collective-permute-start.2
  121.4 4.1 collective-permute-start.5
  126.7 5.1 collective-permute-start.3
  131.8 2.4 fusion.67
  134.2 3.6 collective-permute-done.5
  137.8 5.3 collective-permute-start.6
  143.1 5.9 collective-permute-done.3
  149.0 5.3 collective-permute-start.4
  155.4 297.8 %while.19 = (s32[]{:T(128)}, f32[256,512]{1,0:T(8,128)}, f32[512,256]{1,0:T(8,128)}, f32[2,512,256]{2,1,0:T(8,128)}, s32[]{:T(128)}, /*index=5*/pred[]{:T(512)},...) while((s32[]{:T(128)}, f32[256,512]{1,0:T(8,128)}, ...), condition=%wide.region_9.10_spmd, body=%wide.region_4.9_spmd.sunk | while | flops 5647237120 | bytes 32771136 | solution.py:162
  157.6 17.1 %conditional.2 = (f32[256,512]{1,0:T(8,128)S(1)}, f32[512,256]{1,0:T(8,128)S(1)}, f32[1,512,256]{2,1,0:T(8,128)S(1)}) conditional(s32[]{:T(128)} %convert_element_type.110, (f32[256,512]{1,0:T(8,128)S(1)}, f32[512,256]{1,0:T(8,128)S(1)}) %tuple.60, (bf16[2,512,256]{2,1,0:T(8,128)(2,1)}, s32[]{:T(128)}, bf16[2,512,256]{2,1,0:T(8,128)(2,1)}, ...), branch_computations={%region_5.5_spmd, %region_6.8_spmd} | conditional | flops 5646843904 | bytes 23857272 | solution.py:154
  158.9 2.5 multiply_reduce_fusion.1
  162.2 2.1 multiply_reduce_fusion
  174.7 2.1 collective-permute-start
  176.8 2.1 collective-permute-start.1
  178.9 1.9 select_dynamic-update-slice_fusion.2
  180.8 7.5 %collective-permute-done = f32[256,512]{1,0:T(8,128)} collective-permute-done((f32[256,512]{1,0:T(8,128)S(1)}, f32[256,512]{1,0:T(8,128)}, u32[]{:S(2)}, u32[]{:S(2)}) %collective-permute-start) | collective-permute-done | bytes 524320 | tf_op jit(solution)/shard_map/while/body/eval_jaxpr/ppermute | solution.py:14
  188.3 8.9 %collective-permute-done.1 = f32[512,256]{1,0:T(8,128)} collective-permute-done((f32[512,256]{1,0:T(8,128)S(1)}, f32[512,256]{1,0:T(8,128)}, u32[]{:S(2)}, u32[]{:S(2)}) %collective-permute-start.1) | collective-permute-done | bytes 524320 | tf_op jit(solution)/shard_map/while/body/eval_jaxpr/ppermute | solution.py:14
  199.5 22.3 %collective-permute-start = (f32[256,512]{1,0:T(8,128)S(1)}, f32[256,512]{1,0:T(8,128)}, u32[]{:S(2)}, u32[]{:S(2)}) collective-permute-start(f32[256,512]{1,0:T(8,128)S(1)} %get-tuple-element.431), channel_id=1, source_target_pairs={{0,8},{8,16},{16,24},{1,9},{9,17},{17,25},{2,10},{10,18},{18,26},{... | collective-permute-start | bytes 1572872 | tf_op jit(solution)/shard_map/while/body/eval_jaxpr/ppermute | solution.py:14
  221.8 2.1 collective-permute-start.1
  223.9 1.9 select_dynamic-update-slice_fusion.2
  225.8 7.5 %collective-permute-done = f32[256,512]{1,0:T(8,128)} collective-permute-done((f32[256,512]{1,0:T(8,128)S(1)}, f32[256,512]{1,0:T(8,128)}, u32[]{:S(2)}, u32[]{:S(2)}) %collective-permute-start) | collective-permute-done | bytes 524320 | tf_op jit(solution)/shard_map/while/body/eval_jaxpr/ppermute | solution.py:14
  233.3 8.1 %collective-permute-done.1 = f32[512,256]{1,0:T(8,128)} collective-permute-done((f32[512,256]{1,0:T(8,128)S(1)}, f32[512,256]{1,0:T(8,128)}, u32[]{:S(2)}, u32[]{:S(2)}) %collective-permute-start.1) | collective-permute-done | bytes 524320 | tf_op jit(solution)/shard_map/while/body/eval_jaxpr/ppermute | solution.py:14
  243.7 5.3 collective-permute-start
  249.0 20.1 %collective-permute-start.1 = (f32[512,256]{1,0:T(8,128)S(1)}, f32[512,256]{1,0:T(8,128)}, u32[]{:S(2)}, u32[]{:S(2)}) collective-permute-start(f32[512,256]{1,0:T(8,128)S(1)} %get-tuple-element.432), channel_id=1, source_target_pairs={{0,8},{8,16},{16,24},{1,9},{9,17},{17,25},{2,10},{10,18},{18,26},{... | collective-permute-start | bytes 1572872 | tf_op jit(solution)/shard_map/while/body/eval_jaxpr/ppermute | solution.py:14
  269.1 1.9 select_dynamic-update-slice_fusion.2
  271.0 5.6 collective-permute-done.1
  278.9 12.3 %collective-permute-start = (f32[256,512]{1,0:T(8,128)S(1)}, f32[256,512]{1,0:T(8,128)}, u32[]{:S(2)}, u32[]{:S(2)}) collective-permute-start(f32[256,512]{1,0:T(8,128)S(1)} %get-tuple-element.431), channel_id=1, source_target_pairs={{0,8},{8,16},{16,24},{1,9},{9,17},{17,25},{2,10},{10,18},{18,26},{... | collective-permute-start | bytes 1572872 | tf_op jit(solution)/shard_map/while/body/eval_jaxpr/ppermute | solution.py:14
  291.2 5.4 collective-permute-start.1
  298.5 4.2 collective-permute-done
  302.7 6.7 %collective-permute-done.1 = f32[512,256]{1,0:T(8,128)} collective-permute-done((f32[512,256]{1,0:T(8,128)S(1)}, f32[512,256]{1,0:T(8,128)}, u32[]{:S(2)}, u32[]{:S(2)}) %collective-permute-start.1) | collective-permute-done | bytes 524320 | tf_op jit(solution)/shard_map/while/body/eval_jaxpr/ppermute | solution.py:14
  311.6 17.0 %conditional.2 = (f32[256,512]{1,0:T(8,128)S(1)}, f32[512,256]{1,0:T(8,128)S(1)}, f32[1,512,256]{2,1,0:T(8,128)S(1)}) conditional(s32[]{:T(128)} %convert_element_type.110, (f32[256,512]{1,0:T(8,128)S(1)}, f32[512,256]{1,0:T(8,128)S(1)}) %tuple.60, (bf16[2,512,256]{2,1,0:T(8,128)(2,1)}, s32[]{:T(128)}, bf16[2,512,256]{2,1,0:T(8,128)(2,1)}, ...), branch_computations={%region_5.5_spmd, %region_6.8_spmd} | conditional | flops 5646843904 | bytes 23857272 | solution.py:154
  312.9 2.5 multiply_reduce_fusion.1
  316.2 2.1 multiply_reduce_fusion
  328.7 2.1 collective-permute-start
  330.7 5.7 collective-permute-start.1
  338.4 3.9 collective-permute-done
  342.3 6.1 collective-permute-done.1
  350.7 23.5 %collective-permute-start = (f32[256,512]{1,0:T(8,128)S(1)}, f32[256,512]{1,0:T(8,128)}, u32[]{:S(2)}, u32[]{:S(2)}) collective-permute-start(f32[256,512]{1,0:T(8,128)S(1)} %get-tuple-element.431), channel_id=1, source_target_pairs={{0,8},{8,16},{16,24},{1,9},{9,17},{17,25},{2,10},{10,18},{18,26},{... | collective-permute-start | bytes 1572872 | tf_op jit(solution)/shard_map/while/body/eval_jaxpr/ppermute | solution.py:14
  374.2 2.1 collective-permute-start.1
  378.1 7.1 %collective-permute-done = f32[256,512]{1,0:T(8,128)} collective-permute-done((f32[256,512]{1,0:T(8,128)S(1)}, f32[256,512]{1,0:T(8,128)}, u32[]{:S(2)}, u32[]{:S(2)}) %collective-permute-start) | collective-permute-done | bytes 524320 | tf_op jit(solution)/shard_map/while/body/eval_jaxpr/ppermute | solution.py:14
  385.3 5.6 collective-permute-done.1
  393.2 5.3 collective-permute-start
  398.5 20.1 %collective-permute-start.1 = (f32[512,256]{1,0:T(8,128)S(1)}, f32[512,256]{1,0:T(8,128)}, u32[]{:S(2)}, u32[]{:S(2)}) collective-permute-start(f32[512,256]{1,0:T(8,128)S(1)} %get-tuple-element.432), channel_id=1, source_target_pairs={{0,8},{8,16},{16,24},{1,9},{9,17},{17,25},{2,10},{10,18},{18,26},{... | collective-permute-start | bytes 1572872 | tf_op jit(solution)/shard_map/while/body/eval_jaxpr/ppermute | solution.py:14
  420.5 4.0 collective-permute-done.1
  426.8 11.0 %collective-permute-start = (f32[256,512]{1,0:T(8,128)S(1)}, f32[256,512]{1,0:T(8,128)}, u32[]{:S(2)}, u32[]{:S(2)}) collective-permute-start(f32[256,512]{1,0:T(8,128)S(1)} %get-tuple-element.431), channel_id=1, source_target_pairs={{0,8},{8,16},{16,24},{1,9},{9,17},{17,25},{2,10},{10,18},{18,26},{... | collective-permute-start | bytes 1572872 | tf_op jit(solution)/shard_map/while/body/eval_jaxpr/ppermute | solution.py:14
  437.9 5.4 collective-permute-start.1
  445.2 2.4 collective-permute-done
  447.5 5.6 collective-permute-done.1
  454.8 14.5 %collective-permute-start.7 = (bf16[2,512,256]{2,1,0:T(8,128)(2,1)}, bf16[2,512,256]{2,1,0:T(8,128)(2,1)S(1)}, u32[]{:S(2)}, u32[]{:S(2)}) collective-permute-start(bf16[2,512,256]{2,1,0:T(8,128)(2,1)} %collective-permute-done.6), channel_id=1, source_target_pairs={{0,8},{8,16},{16,24},{1,9},{9,17},{17,25},{2,10},{10,18},{18,26},{... | collective-permute-start | bytes 1572872 | tf_op jit(solution)/shard_map/ppermute | solution.py:14
  471.2 1.9 constant_dynamic-update-slice_fusion.2
  473.9 2.0 constant_dynamic-update-slice_fusion
  479.8 5.6 fusion.81
  485.5 8.3 %fusion.70 = bf16[2,512,256]{2,1,0:T(8,128)(2,1)} fusion(bf16[2,2560,256]{2,1,0:T(8,128)(2,1)} %copy-done.14, f32[2,512]{1,0:T(2,128)S(1)} %fusion.81, f32[2,512,256]{2,1,0:T(8,128)S(1)} %copy-done.2, f32[256]{0:T(256)S(1)} %bitcast.85, f32[2,512]{1,0:T(2,128)S(1)} %add_rsqrt_fusion, f32[]{:T(128)} %bitcast.72, pred[512,2560]{1,0:T(8,128)(4,1)} %fusion.67, ...), kind=kOutput, calls=%fused_computation.84 | convolution fusion | flops 2698513920 | bytes 8659972 | tf_op jit(solution)/shard_map/sqk,skd->sqd/dot_general | solution.py:84
  493.8 7.3 %copy.11 = bf16[1,256,4096]{1,0,2:T(2,128)(2,1)} copy(bf16[1,256,4096]{2,1,0:T(8,128)(2,1)S(1)} %copy-done.5) | data formatting | bytes 4194304 | tf_op args[7]
  501.7 21.6 %reduce = bf16[4096,256]{1,0:T(8,128)(2,1)S(1)} reduce(bf16[4096,1,256]{2,1,0:T(2,128)(2,1)} %bitcast.74, bf16[]{:T(256)} %broadcast.150), dimensions={1}, to_apply=%bitcast.36.reduce_sub_computation | reduce | bytes 4194306
  523.4 3.3 reshape.120
  526.6 65.8 %all_to_all.15 = bf16[8,2,65536]{2,1,0:T(2,128)(2,1)S(1)} all-to-all(bf16[8,2,65536]{2,1,0:T(2,128)(2,1)} %reshape.120), channel_id=1, replica_groups=mesh['seq'=4,'head'=8] {'head'}, dimensions={0} | all-to-all | bytes 4194304 | tf_op jit(solution)/shard_map/all_to_all | solution.py:166
  592.4 4.4 reshape.121
  596.8 2.5 copy.13
  599.4 2.4 copy.12
  601.8 6.2 %convolution_convert_fusion = bf16[1024,512]{1,0:T(8,128)(2,1)} fusion(bf16[1024,2048]{1,0:T(8,128)(2,1)} %all-gather.5.cloned.1.call-done, bf16[2048,512]{1,0:T(8,128)(2,1)} %bitcast.77), kind=kOutput, calls=%fused_computation.82 | convolution fusion | flops 2148007936 | bytes 7340032 | tf_op jit(solution)/shard_map/dot_general | solution.py:168
  (127 shorter events, 70.1 us)
Async XLA Ops:
  6.5 87.2 %copy-start = (bf16[4096,1]{0,1:T(2,128)(2,1)S(1)}, bf16[4096,1]{0,1:T(2,128)(2,1)}, u32[]{:S(2)}) copy-start(bf16[4096,1]{0,1:T(2,128)(2,1)} %param.14) | copy-start | bytes 24580
  6.5 87.2 %all-gather.3.cloned.1.call-start = ((), (), s32[]{:S(2)}) async-start(), calls=%async_computation.1 | async-start | bytes 9437184 | tf_op jit(solution)/shard_map/all_gather | solution.py:109
  7.3 594.5 %all-gather.5.cloned.1.call-start = ((), (), s32[]{:S(2)}) async-start(), calls=%async_computation.2 | async-start | bytes 4718592 | tf_op jit(solution)/shard_map/all_gather | solution.py:169
  93.7 5.8 copy-start.3
  108.5 2.1 copy-start.4
  110.7 16.0 %collective-permute-start.2 = (bf16[2,512,256]{2,1,0:T(8,128)(2,1)}, bf16[2,512,256]{2,1,0:T(8,128)(2,1)S(1)}, u32[]{:S(2)}, u32[]{:S(2)}) collective-permute-start(bf16[2,512,256]{2,1,0:T(8,128)(2,1)} %bitcast.8), channel_id=1, source_target_pairs={{0,8},{8,16},{16,24},{1,9},{9,17},{17,25},{2,10},{10,18},{18,26},{... | collective-permute-start | bytes 1572872 | tf_op jit(solution)/shard_map/ppermute | solution.py:14
  121.4 33.9 %copy-start.6 = (bf16[1024,256]{1,0:T(8,128)(2,1)}, bf16[1024,256]{1,0:T(8,128)(2,1)S(1)}, u32[]{:S(2)}) copy-start(bf16[1024,256]{1,0:T(8,128)(2,1)S(1)} %slice.21) | copy-start | bytes 1572868
  121.4 16.4 %collective-permute-start.5 = (bf16[2,512,256]{2,1,0:T(8,128)(2,1)S(1)}, bf16[2,512,256]{2,1,0:T(8,128)(2,1)}, u32[]{:S(2)}, u32[]{:S(2)}) collective-permute-start(bf16[2,512,256]{2,1,0:T(8,128)(2,1)S(1)} %bitcast.78), channel_id=1, source_target_pairs={{0,8},{8,16},{16,24},{1,9},{9,17},{17,25},{2,10},{10,18},{18,26},{... | collective-permute-start | bytes 1572872 | tf_op jit(solution)/shard_map/ppermute | solution.py:14
  126.7 28.7 %copy-start.9 = (bf16[2,512,256]{2,1,0:T(8,128)(2,1)}, bf16[2,512,256]{2,1,0:T(8,128)(2,1)S(1)}, u32[]{:S(2)}) copy-start(bf16[2,512,256]{2,1,0:T(8,128)(2,1)S(1)} %collective-permute-done.2) | copy-start | bytes 1572868
  126.7 22.4 %collective-permute-start.3 = (bf16[2,512,256]{2,1,0:T(8,128)(2,1)S(1)}, bf16[2,512,256]{2,1,0:T(8,128)(2,1)}, u32[]{:S(2)}, u32[]{:S(2)}) collective-permute-start(bf16[2,512,256]{2,1,0:T(8,128)(2,1)S(1)} %collective-permute-done.2), channel_id=1, source_target_pairs={{0,8},{8,16},{16,24},{1,9},{9,17},{17,25},{2,10},{10,18},{18,26},{... | collective-permute-start | bytes 1572872 | tf_op jit(solution)/shard_map/ppermute | solution.py:14
  137.8 316.9 %collective-permute-start.6 = (bf16[2,512,256]{2,1,0:T(8,128)(2,1)}, bf16[2,512,256]{2,1,0:T(8,128)(2,1)}, u32[]{:S(2)}, u32[]{:S(2)}) collective-permute-start(bf16[2,512,256]{2,1,0:T(8,128)(2,1)} %collective-permute-done.5), channel_id=1, source_target_pairs={{0,8},{8,16},{16,24},{1,9},{9,17},{17,25},{2,10},{10,18},{18,26},{... | collective-permute-start | bytes 1572872 | tf_op jit(solution)/shard_map/ppermute | solution.py:14
  149.0 320.3 %collective-permute-start.4 = (bf16[2,512,256]{2,1,0:T(8,128)(2,1)}, bf16[2,512,256]{2,1,0:T(8,128)(2,1)}, u32[]{:S(2)}, u32[]{:S(2)}) collective-permute-start(bf16[2,512,256]{2,1,0:T(8,128)(2,1)} %collective-permute-done.3), channel_id=1, source_target_pairs={{0,8},{8,16},{16,24},{1,9},{9,17},{17,25},{2,10},{10,18},{18,26},{... | collective-permute-start | bytes 1572872 | tf_op jit(solution)/shard_map/ppermute | solution.py:14
  170.6 3.5 copy-start.11
  174.7 13.6 %collective-permute-start = (f32[256,512]{1,0:T(8,128)S(1)}, f32[256,512]{1,0:T(8,128)}, u32[]{:S(2)}, u32[]{:S(2)}) collective-permute-start(f32[256,512]{1,0:T(8,128)S(1)} %get-tuple-element.431), channel_id=1, source_target_pairs={{0,8},{8,16},{16,24},{1,9},{9,17},{17,25},{2,10},{10,18},{18,26},{... | collective-permute-start | bytes 1572872 | tf_op jit(solution)/shard_map/while/body/eval_jaxpr/ppermute | solution.py:14
  176.8 20.4 %collective-permute-start.1 = (f32[512,256]{1,0:T(8,128)S(1)}, f32[512,256]{1,0:T(8,128)}, u32[]{:S(2)}, u32[]{:S(2)}) collective-permute-start(f32[512,256]{1,0:T(8,128)S(1)} %get-tuple-element.432), channel_id=1, source_target_pairs={{0,8},{8,16},{16,24},{1,9},{9,17},{17,25},{2,10},{10,18},{18,26},{... | collective-permute-start | bytes 1572872 | tf_op jit(solution)/shard_map/while/body/eval_jaxpr/ppermute | solution.py:14
  199.5 33.8 %collective-permute-start = (f32[256,512]{1,0:T(8,128)S(1)}, f32[256,512]{1,0:T(8,128)}, u32[]{:S(2)}, u32[]{:S(2)}) collective-permute-start(f32[256,512]{1,0:T(8,128)S(1)} %get-tuple-element.431), channel_id=1, source_target_pairs={{0,8},{8,16},{16,24},{1,9},{9,17},{17,25},{2,10},{10,18},{18,26},{... | collective-permute-start | bytes 1572872 | tf_op jit(solution)/shard_map/while/body/eval_jaxpr/ppermute | solution.py:14
  221.8 19.6 %collective-permute-start.1 = (f32[512,256]{1,0:T(8,128)S(1)}, f32[512,256]{1,0:T(8,128)}, u32[]{:S(2)}, u32[]{:S(2)}) collective-permute-start(f32[512,256]{1,0:T(8,128)S(1)} %get-tuple-element.432), channel_id=1, source_target_pairs={{0,8},{8,16},{16,24},{1,9},{9,17},{17,25},{2,10},{10,18},{18,26},{... | collective-permute-start | bytes 1572872 | tf_op jit(solution)/shard_map/while/body/eval_jaxpr/ppermute | solution.py:14
  243.7 27.3 %collective-permute-start = (f32[256,512]{1,0:T(8,128)S(1)}, f32[256,512]{1,0:T(8,128)}, u32[]{:S(2)}, u32[]{:S(2)}) collective-permute-start(f32[256,512]{1,0:T(8,128)S(1)} %get-tuple-element.431), channel_id=1, source_target_pairs={{0,8},{8,16},{16,24},{1,9},{9,17},{17,25},{2,10},{10,18},{18,26},{... | collective-permute-start | bytes 1572872 | tf_op jit(solution)/shard_map/while/body/eval_jaxpr/ppermute | solution.py:14
  249.0 27.6 %collective-permute-start.1 = (f32[512,256]{1,0:T(8,128)S(1)}, f32[512,256]{1,0:T(8,128)}, u32[]{:S(2)}, u32[]{:S(2)}) collective-permute-start(f32[512,256]{1,0:T(8,128)S(1)} %get-tuple-element.432), channel_id=1, source_target_pairs={{0,8},{8,16},{16,24},{1,9},{9,17},{17,25},{2,10},{10,18},{18,26},{... | collective-permute-start | bytes 1572872 | tf_op jit(solution)/shard_map/while/body/eval_jaxpr/ppermute | solution.py:14
  278.9 23.8 %collective-permute-start = (f32[256,512]{1,0:T(8,128)S(1)}, f32[256,512]{1,0:T(8,128)}, u32[]{:S(2)}, u32[]{:S(2)}) collective-permute-start(f32[256,512]{1,0:T(8,128)S(1)} %get-tuple-element.431), channel_id=1, source_target_pairs={{0,8},{8,16},{16,24},{1,9},{9,17},{17,25},{2,10},{10,18},{18,26},{... | collective-permute-start | bytes 1572872 | tf_op jit(solution)/shard_map/while/body/eval_jaxpr/ppermute | solution.py:14
  291.2 18.2 %collective-permute-start.1 = (f32[512,256]{1,0:T(8,128)S(1)}, f32[512,256]{1,0:T(8,128)}, u32[]{:S(2)}, u32[]{:S(2)}) collective-permute-start(f32[512,256]{1,0:T(8,128)S(1)} %get-tuple-element.432), channel_id=1, source_target_pairs={{0,8},{8,16},{16,24},{1,9},{9,17},{17,25},{2,10},{10,18},{18,26},{... | collective-permute-start | bytes 1572872 | tf_op jit(solution)/shard_map/while/body/eval_jaxpr/ppermute | solution.py:14
  324.6 3.5 copy-start.11
  328.7 13.6 %collective-permute-start = (f32[256,512]{1,0:T(8,128)S(1)}, f32[256,512]{1,0:T(8,128)}, u32[]{:S(2)}, u32[]{:S(2)}) collective-permute-start(f32[256,512]{1,0:T(8,128)S(1)} %get-tuple-element.431), channel_id=1, source_target_pairs={{0,8},{8,16},{16,24},{1,9},{9,17},{17,25},{2,10},{10,18},{18,26},{... | collective-permute-start | bytes 1572872 | tf_op jit(solution)/shard_map/while/body/eval_jaxpr/ppermute | solution.py:14
  330.7 17.6 %collective-permute-start.1 = (f32[512,256]{1,0:T(8,128)S(1)}, f32[512,256]{1,0:T(8,128)}, u32[]{:S(2)}, u32[]{:S(2)}) collective-permute-start(f32[512,256]{1,0:T(8,128)S(1)} %get-tuple-element.432), channel_id=1, source_target_pairs={{0,8},{8,16},{16,24},{1,9},{9,17},{17,25},{2,10},{10,18},{18,26},{... | collective-permute-start | bytes 1572872 | tf_op jit(solution)/shard_map/while/body/eval_jaxpr/ppermute | solution.py:14
  350.7 34.6 %collective-permute-start = (f32[256,512]{1,0:T(8,128)S(1)}, f32[256,512]{1,0:T(8,128)}, u32[]{:S(2)}, u32[]{:S(2)}) collective-permute-start(f32[256,512]{1,0:T(8,128)S(1)} %get-tuple-element.431), channel_id=1, source_target_pairs={{0,8},{8,16},{16,24},{1,9},{9,17},{17,25},{2,10},{10,18},{18,26},{... | collective-permute-start | bytes 1572872 | tf_op jit(solution)/shard_map/while/body/eval_jaxpr/ppermute | solution.py:14
  374.2 16.7 %collective-permute-start.1 = (f32[512,256]{1,0:T(8,128)S(1)}, f32[512,256]{1,0:T(8,128)}, u32[]{:S(2)}, u32[]{:S(2)}) collective-permute-start(f32[512,256]{1,0:T(8,128)S(1)} %get-tuple-element.432), channel_id=1, source_target_pairs={{0,8},{8,16},{16,24},{1,9},{9,17},{17,25},{2,10},{10,18},{18,26},{... | collective-permute-start | bytes 1572872 | tf_op jit(solution)/shard_map/while/body/eval_jaxpr/ppermute | solution.py:14
  393.2 27.3 %collective-permute-start = (f32[256,512]{1,0:T(8,128)S(1)}, f32[256,512]{1,0:T(8,128)}, u32[]{:S(2)}, u32[]{:S(2)}) collective-permute-start(f32[256,512]{1,0:T(8,128)S(1)} %get-tuple-element.431), channel_id=1, source_target_pairs={{0,8},{8,16},{16,24},{1,9},{9,17},{17,25},{2,10},{10,18},{18,26},{... | collective-permute-start | bytes 1572872 | tf_op jit(solution)/shard_map/while/body/eval_jaxpr/ppermute | solution.py:14
  398.5 26.0 %collective-permute-start.1 = (f32[512,256]{1,0:T(8,128)S(1)}, f32[512,256]{1,0:T(8,128)}, u32[]{:S(2)}, u32[]{:S(2)}) collective-permute-start(f32[512,256]{1,0:T(8,128)S(1)} %get-tuple-element.432), channel_id=1, source_target_pairs={{0,8},{8,16},{16,24},{1,9},{9,17},{17,25},{2,10},{10,18},{18,26},{... | collective-permute-start | bytes 1572872 | tf_op jit(solution)/shard_map/while/body/eval_jaxpr/ppermute | solution.py:14
  426.8 20.7 %collective-permute-start = (f32[256,512]{1,0:T(8,128)S(1)}, f32[256,512]{1,0:T(8,128)}, u32[]{:S(2)}, u32[]{:S(2)}) collective-permute-start(f32[256,512]{1,0:T(8,128)S(1)} %get-tuple-element.431), channel_id=1, source_target_pairs={{0,8},{8,16},{16,24},{1,9},{9,17},{17,25},{2,10},{10,18},{18,26},{... | collective-permute-start | bytes 1572872 | tf_op jit(solution)/shard_map/while/body/eval_jaxpr/ppermute | solution.py:14
  437.9 15.3 %collective-permute-start.1 = (f32[512,256]{1,0:T(8,128)S(1)}, f32[512,256]{1,0:T(8,128)}, u32[]{:S(2)}, u32[]{:S(2)}) collective-permute-start(f32[512,256]{1,0:T(8,128)S(1)} %get-tuple-element.432), channel_id=1, source_target_pairs={{0,8},{8,16},{16,24},{1,9},{9,17},{17,25},{2,10},{10,18},{18,26},{... | collective-permute-start | bytes 1572872 | tf_op jit(solution)/shard_map/while/body/eval_jaxpr/ppermute | solution.py:14
  453.1 19.9 %copy-start.10 = (bf16[2,512,256]{2,1,0:T(8,128)(2,1)S(1)}, bf16[2,512,256]{2,1,0:T(8,128)(2,1)}, u32[]{:S(2)}) copy-start(bf16[2,512,256]{2,1,0:T(8,128)(2,1)} %copy-done.9) | copy-start | bytes 1572868
  453.1 22.9 %copy-start.13 = (bf16[2,2560,256]{2,1,0:T(8,128)(2,1)S(1)}, bf16[2,2560,256]{2,1,0:T(8,128)(2,1)}, u32[]{:S(2)}) copy-start(bf16[2,2560,256]{2,1,0:T(8,128)(2,1)} %broadcast_dynamic-update-slice_fusion) | copy-start | bytes 7864324
  454.8 21.3 %collective-permute-start.7 = (bf16[2,512,256]{2,1,0:T(8,128)(2,1)}, bf16[2,512,256]{2,1,0:T(8,128)(2,1)S(1)}, u32[]{:S(2)}, u32[]{:S(2)}) collective-permute-start(bf16[2,512,256]{2,1,0:T(8,128)(2,1)} %collective-permute-done.6), channel_id=1, source_target_pairs={{0,8},{8,16},{16,24},{1,9},{9,17},{17,25},{2,10},{10,18},{18,26},{... | collective-permute-start | bytes 1572872 | tf_op jit(solution)/shard_map/ppermute | solution.py:14
  473.1 5.2 copy-start.7
  473.9 5.9 copy-start.8
  473.9 5.9 copy-start.12
  478.3 1.5 copy-start.14
  479.8 5.6 copy-start.2
  479.8 5.7 copy-start.15
  485.5 8.3 %copy-start.5 = (bf16[1,256,4096]{2,1,0:T(8,128)(2,1)S(1)}, bf16[1,256,4096]{2,1,0:T(8,128)(2,1)}, u32[]{:S(2)}) copy-start(bf16[1,256,4096]{2,1,0:T(8,128)(2,1)} %param.19) | copy-start | bytes 6291460
  601.8 6.2 %copy-start.1 = (bf16[4096,1]{0,1:T(2,128)(2,1)S(1)}, bf16[4096,1]{0,1:T(2,128)(2,1)}, u32[]{:S(2)}) copy-start(bf16[4096,1]{0,1:T(2,128)(2,1)} %param.14) | copy-start | bytes 24580
Sparse Core Ops, SparseCore 0:
  8.9 84.7 all-gather.2
  494.0 77.1 all-gather.4
where the time goes:
time: 617 us; the launch traced here: 615 us
  starting transfers between devices  185 us (30%)
  waiting for transfers between devices  181 us (29%)
  blocking collectives  65.8 us (11%)
  matrix products  65.7 us (11%)
  other arithmetic  60.9 us (10%)
  local copies, waits for them, and re-layouts  38.9 us (6%)
  between operations  14.3 us (2%)
    ppermute x22, starting transfers between devices, shifted(): return lax.ppermute(block, axis, route)  185 us
    ppermute x22, waiting for transfers between devices, shifted(): return lax.ppermute(block, axis, route)  93.9 us
    all_gather x1, waiting for transfers between devices, body(): piece = lax.all_gather(flattened, 'head', axis=1, tiled=True)  86.4 us
    all_to_all x1, blocking collectives, body(): lax.all_to_all(final_mixing_matrix, 'head', split_axis=2, concat_axis=0,...  65.8 us
    unnamed x45, local copies, waits for them, and re-layouts  31.9 us
    unnamed x1, other arithmetic  21.6 us
    select_n x8, other arithmetic, turn(): fast_all = jnp.where(live, stored, fast_all)  15.2 us
  transfers between devices with their start and end apart: 24, of which 19 were waited for; matrix products, arithmetic and copies ran while one was open for 20% of the time, Pallas kernels for 0%

commit v1 on v0

--- a/solution.py
+++ b/solution.py
@@ -6,6 +6,12 @@
 WIN = 2048
 NS_STEPS = 3
 update_rate = 0.3
+
+
+def swap_blocks(x, mesh_axis, split, join):
+    shards = jnp.split(x, lax.axis_size(mesh_axis), axis=split)
+    arrived = lax.all_to_all(jnp.stack(shards), mesh_axis, 0, 0)
+    return jnp.concatenate(arrived, axis=join)
 
 
 def shifted(block, axis, distance):
@@ -163,7 +169,7 @@
     head_out = combine(attended_output, carried[2], adapter_gain_vector[0]).reshape(
         total_rows, head_dim
     )
-    columns = lax.all_to_all(final_mixing_matrix, "head", split_axis=2, concat_axis=0, tiled=True)
+    columns = swap_blocks(final_mixing_matrix, "head", 2, 0)
     columns = columns.reshape(-1, columns.shape[2])
     result = jnp.dot(
         lax.all_gather(head_out, "head", axis=1, tiled=True),

time: 617 us -> 594 us (0.963)
  other arithmetic: 60.9 us -> 30.8 us
  local copies, waits for them, and re-layouts: 38.9 us -> 18.7 us
  blocking collectives: 65.8 us -> 85.2 us
  waiting for transfers between devices: 181 us -> 191 us
    unnamed x1 -> x0, other arithmetic: 21.6 us -> none
    all_to_all x1, blocking collectives: 65.8 us -> 85.2 us  [swap_blocks(): arrived = lax.all_to_all(jnp.stack(shards), mesh_axis, 0, 0)]
    unnamed x45 -> x47, local copies, waits for them, and re-layouts: 31.9 us -> 12.8 us
    ppermute x22, waiting for transfers between devices: 93.9 us -> 103 us  [shifted(): return lax.ppermute(block, axis, route)]
    select_n x8, other arithmetic: 9.06 us -> 0.66 us  [turn(): use_in = jnp.where(token_position == 0, start_in, held_in)]
  transfers between devices with their start and end apart: 24 -> 24, of which waited for: 19 -> 20; matrix products, arithmetic and copies ran while one was open for 20% -> 13% of each run, Pallas kernels for 0% -> 0%
where the time goes in v1:
time: 594 us; the launch traced here: 586 us
  waiting for transfers between devices  191 us (32%)
  starting transfers between devices  179 us (30%)
  blocking collectives  85.2 us (14%)
  matrix products  64.3 us (11%)
  other arithmetic  30.8 us (5%)
  local copies, waits for them, and re-layouts  18.7 us (3%)
  between operations  14.3 us (2%)
    ppermute x22, starting transfers between devices, shifted(): return lax.ppermute(block, axis, route)  179 us
    ppermute x22, waiting for transfers between devices, shifted(): return lax.ppermute(block, axis, route)  103 us
    all_gather x1, waiting for transfers between devices, body(): piece = lax.all_gather(flattened, 'head', axis=1, tiled=True)  86.4 us
    all_to_all x1, blocking collectives, swap_blocks(): arrived = lax.all_to_all(jnp.stack(shards), mesh_axis, 0, 0)  85.2 us
    select_n x8, other arithmetic, turn(): fast_all = jnp.where(live, stored, fast_all)  15.3 us
    unnamed x47, local copies, waits for them, and re-layouts  12.8 us
  transfers between devices with their start and end apart: 24, of which 20 were waited for; matrix products, arithmetic and copies ran while one was open for 13% of the time, Pallas kernels for 0%

profile of v1, /device:TPU:0, one launch (start us, length us, event | category | flops | bytes accessed | tf_op | source)
XLA Modules:
  0.0 586.5 jit_solution(16104880725078889459)
XLA Ops:
  7.3 86.4 %all-gather.3.cloned.1.call-done = bf16[1024,4096]{1,0:T(8,128)(2,1)} async-done(((bf16[1024,512]{1,0:T(8,128)(2,1)}), bf16[1024,4096]{1,0:T(8,128)(2,1)}) %all-gather.3.cloned.1.call-update) | async-done | bytes 8388624 | tf_op jit(solution)/shard_map/all_gather | solution.py:115
  93.7 11.0 %fusion.61 = f32[1024,768]{1,0:T(8,128)S(1)} fusion(bf16[1024,4096]{1,0:T(8,128)(2,1)} %all-gather.3.cloned.1.call-done, bf16[4096,1,768]{2,0,1:T(8,128)(2,1)} %param.13), kind=kOutput, calls=%fused_computation.72 | convolution fusion | flops 6442450944 | bytes 17825792 | tf_op jit(solution)/shard_map/dot_general | solution.py:116
  105.2 2.3 fusion.86
  107.5 1.6 multiply_convert_fusion.3
  109.1 3.4 collective-permute-start.2
  118.8 4.2 collective-permute-start.5
  123.0 2.1 collective-permute-done.2
  125.1 5.1 collective-permute-start.3
  130.1 2.4 fusion.67
  132.5 3.7 collective-permute-done.5
  136.2 5.3 collective-permute-start.6
  141.5 5.9 %collective-permute-done.3 = bf16[2,512,256]{2,1,0:T(8,128)(2,1)} collective-permute-done((bf16[2,512,256]{2,1,0:T(8,128)(2,1)S(1)}, bf16[2,512,256]{2,1,0:T(8,128)(2,1)}, u32[]{:S(2)}, u32[]{:S(2)}) %collective-permute-start.3) | collective-permute-done | bytes 524320 | tf_op jit(solution)/shard_map/ppermute | solution.py:20
  147.4 5.3 collective-permute-start.4
  153.8 292.6 %while.19 = (s32[]{:T(128)}, f32[256,512]{1,0:T(8,128)}, f32[512,256]{1,0:T(8,128)S(1)}, f32[2,512,256]{2,1,0:T(8,128)}, s32[]{:T(128)}, /*index=5*/pred[]{:T(51...) while((s32[]{:T(128)}, f32[256,512]{1,0:T(8,128)}, ...), condition=%wide.region_9.10_spmd, body=%wide.region_4.9_spmd.sunk | while | flops 5647237120 | bytes 39062676 | solution.py:168
  155.0 17.6 %conditional.2 = (f32[256,512]{1,0:T(8,128)S(1)}, f32[512,256]{1,0:T(8,128)S(1)}, f32[1,512,256]{2,1,0:T(8,128)S(1)}) conditional(s32[]{:T(128)} %convert_element_type.110, (f32[256,512]{1,0:T(8,128)S(1)}, f32[512,256]{1,0:T(8,128)S(1)}) %tuple.60, (bf16[2,512,256]{2,1,0:T(8,128)(2,1)}, s32[]{:T(128)}, bf16[2,512,256]{2,1,0:T(8,128)(2,1)}, ...), branch_computations={%region_5.5_spmd, %region_6.8_spmd} | conditional | flops 5646843904 | bytes 28051632 | solution.py:160
  156.3 2.0 multiply_reduce_fusion
  164.6 2.4 multiply_reduce_fusion.1
  172.6 2.1 collective-permute-start
  176.0 1.9 select_dynamic-update-slice_fusion.2
  177.9 8.3 %collective-permute-done = f32[256,512]{1,0:T(8,128)} collective-permute-done((f32[256,512]{1,0:T(8,128)S(1)}, f32[256,512]{1,0:T(8,128)}, u32[]{:S(2)}, u32[]{:S(2)}) %collective-permute-start) | collective-permute-done | bytes 524320 | tf_op jit(solution)/shard_map/while/body/eval_jaxpr/ppermute | solution.py:20
  186.2 9.0 %collective-permute-done.1 = f32[512,256]{1,0:T(8,128)S(1)} collective-permute-done((f32[512,256]{1,0:T(8,128)}, f32[512,256]{1,0:T(8,128)S(1)}, u32[]{:S(2)}, u32[]{:S(2)}) %collective-permute-start.1) | collective-permute-done | bytes 524320 | tf_op jit(solution)/shard_map/while/body/eval_jaxpr/ppermute | solution.py:20
  196.5 22.6 %collective-permute-start = (f32[256,512]{1,0:T(8,128)S(1)}, f32[256,512]{1,0:T(8,128)}, u32[]{:S(2)}, u32[]{:S(2)}) collective-permute-start(f32[256,512]{1,0:T(8,128)S(1)} %get-tuple-element.431), channel_id=1, source_target_pairs={{0,8},{8,16},{16,24},{1,9},{9,17},{17,25},{2,10},{10,18},{18,26},{... | collective-permute-start | bytes 1572872 | tf_op jit(solution)/shard_map/while/body/eval_jaxpr/ppermute | solution.py:20
  220.4 1.9 select_dynamic-update-slice_fusion.2
  222.3 8.3 %collective-permute-done = f32[256,512]{1,0:T(8,128)} collective-permute-done((f32[256,512]{1,0:T(8,128)S(1)}, f32[256,512]{1,0:T(8,128)}, u32[]{:S(2)}, u32[]{:S(2)}) %collective-permute-start) | collective-permute-done | bytes 524320 | tf_op jit(solution)/shard_map/while/body/eval_jaxpr/ppermute | solution.py:20
  230.6 8.1 %collective-permute-done.1 = f32[512,256]{1,0:T(8,128)S(1)} collective-permute-done((f32[512,256]{1,0:T(8,128)}, f32[512,256]{1,0:T(8,128)S(1)}, u32[]{:S(2)}, u32[]{:S(2)}) %collective-permute-start.1) | collective-permute-done | bytes 524320 | tf_op jit(solution)/shard_map/while/body/eval_jaxpr/ppermute | solution.py:20
  240.0 5.1 collective-permute-start
  245.1 19.8 %collective-permute-start.1 = (f32[512,256]{1,0:T(8,128)}, f32[512,256]{1,0:T(8,128)S(1)}, u32[]{:S(2)}, u32[]{:S(2)}) collective-permute-start(f32[512,256]{1,0:T(8,128)} %copy-done.5), channel_id=1, source_target_pairs={{0,8},{8,16},{16,24},{1,9},{9,17},{17,25},{2,10},{10,18},{18,26},{... | collective-permute-start | bytes 1572872 | tf_op jit(solution)/shard_map/while/body/eval_jaxpr/ppermute | solution.py:20
  264.9 1.9 select_dynamic-update-slice_fusion.2
  266.9 6.6 %collective-permute-done.1 = f32[512,256]{1,0:T(8,128)S(1)} collective-permute-done((f32[512,256]{1,0:T(8,128)}, f32[512,256]{1,0:T(8,128)S(1)}, u32[]{:S(2)}, u32[]{:S(2)}) %collective-permute-start.1) | collective-permute-done | bytes 524320 | tf_op jit(solution)/shard_map/while/body/eval_jaxpr/ppermute | solution.py:20
  274.8 12.1 %collective-permute-start = (f32[256,512]{1,0:T(8,128)S(1)}, f32[256,512]{1,0:T(8,128)}, u32[]{:S(2)}, u32[]{:S(2)}) collective-permute-start(f32[256,512]{1,0:T(8,128)S(1)} %get-tuple-element.431), channel_id=1, source_target_pairs={{0,8},{8,16},{16,24},{1,9},{9,17},{17,25},{2,10},{10,18},{18,26},{... | collective-permute-start | bytes 1572872 | tf_op jit(solution)/shard_map/while/body/eval_jaxpr/ppermute | solution.py:20
  286.9 4.4 collective-permute-start.1
  291.3 1.9 select_dynamic-update-slice_fusion.2
  293.2 5.2 collective-permute-done
  298.4 6.7 %collective-permute-done.1 = f32[512,256]{1,0:T(8,128)S(1)} collective-permute-done((f32[512,256]{1,0:T(8,128)}, f32[512,256]{1,0:T(8,128)S(1)}, u32[]{:S(2)}, u32[]{:S(2)}) %collective-permute-start.1) | collective-permute-done | bytes 524320 | tf_op jit(solution)/shard_map/while/body/eval_jaxpr/ppermute | solution.py:20
  306.3 17.6 %conditional.2 = (f32[256,512]{1,0:T(8,128)S(1)}, f32[512,256]{1,0:T(8,128)S(1)}, f32[1,512,256]{2,1,0:T(8,128)S(1)}) conditional(s32[]{:T(128)} %convert_element_type.110, (f32[256,512]{1,0:T(8,128)S(1)}, f32[512,256]{1,0:T(8,128)S(1)}) %tuple.60, (bf16[2,512,256]{2,1,0:T(8,128)(2,1)}, s32[]{:T(128)}, bf16[2,512,256]{2,1,0:T(8,128)(2,1)}, ...), branch_computations={%region_5.5_spmd, %region_6.8_spmd} | conditional | flops 5646843904 | bytes 28051632 | solution.py:160
  307.6 2.0 multiply_reduce_fusion
  315.9 2.4 multiply_reduce_fusion.1
  323.9 2.1 collective-permute-start
  326.0 4.7 collective-permute-start.1
  330.7 1.9 select_dynamic-update-slice_fusion.2
  332.6 4.9 collective-permute-done
  337.5 6.1 %collective-permute-done.1 = f32[512,256]{1,0:T(8,128)S(1)} collective-permute-done((f32[512,256]{1,0:T(8,128)}, f32[512,256]{1,0:T(8,128)S(1)}, u32[]{:S(2)}, u32[]{:S(2)}) %collective-permute-start.1) | collective-permute-done | bytes 524320 | tf_op jit(solution)/shard_map/while/body/eval_jaxpr/ppermute | solution.py:20
  345.0 23.8 %collective-permute-start = (f32[256,512]{1,0:T(8,128)S(1)}, f32[256,512]{1,0:T(8,128)}, u32[]{:S(2)}, u32[]{:S(2)}) collective-permute-start(f32[256,512]{1,0:T(8,128)S(1)} %get-tuple-element.431), channel_id=1, source_target_pairs={{0,8},{8,16},{16,24},{1,9},{9,17},{17,25},{2,10},{10,18},{18,26},{... | collective-permute-start | bytes 1572872 | tf_op jit(solution)/shard_map/while/body/eval_jaxpr/ppermute | solution.py:20
  370.1 1.9 select_dynamic-update-slice_fusion.2
  372.0 7.8 %collective-permute-done = f32[256,512]{1,0:T(8,128)} collective-permute-done((f32[256,512]{1,0:T(8,128)S(1)}, f32[256,512]{1,0:T(8,128)}, u32[]{:S(2)}, u32[]{:S(2)}) %collective-permute-start) | collective-permute-done | bytes 524320 | tf_op jit(solution)/shard_map/while/body/eval_jaxpr/ppermute | solution.py:20
  379.8 5.7 collective-permute-done.1
  386.8 5.1 collective-permute-start
  392.0 19.8 %collective-permute-start.1 = (f32[512,256]{1,0:T(8,128)}, f32[512,256]{1,0:T(8,128)S(1)}, u32[]{:S(2)}, u32[]{:S(2)}) collective-permute-start(f32[512,256]{1,0:T(8,128)} %copy-done.5), channel_id=1, source_target_pairs={{0,8},{8,16},{16,24},{1,9},{9,17},{17,25},{2,10},{10,18},{18,26},{... | collective-permute-start | bytes 1572872 | tf_op jit(solution)/shard_map/while/body/eval_jaxpr/ppermute | solution.py:20
  411.7 1.9 select_dynamic-update-slice_fusion.2
  413.7 5.1 collective-permute-done.1
  420.0 10.9 %collective-permute-start = (f32[256,512]{1,0:T(8,128)S(1)}, f32[256,512]{1,0:T(8,128)}, u32[]{:S(2)}, u32[]{:S(2)}) collective-permute-start(f32[256,512]{1,0:T(8,128)S(1)} %get-tuple-element.431), channel_id=1, source_target_pairs={{0,8},{8,16},{16,24},{1,9},{9,17},{17,25},{2,10},{10,18},{18,26},{... | collective-permute-start | bytes 1572872 | tf_op jit(solution)/shard_map/while/body/eval_jaxpr/ppermute | solution.py:20
  431.0 4.4 collective-permute-start.1
  435.4 1.9 select_dynamic-update-slice_fusion.2
  437.3 3.4 collective-permute-done
  440.7 5.7 collective-permute-done.1
  446.4 1.6 multiply_reduce_fusion.2
  448.0 15.0 %collective-permute-start.7 = (bf16[2,512,256]{2,1,0:T(8,128)(2,1)}, bf16[2,512,256]{2,1,0:T(8,128)(2,1)S(1)}, u32[]{:S(2)}, u32[]{:S(2)}) collective-permute-start(bf16[2,512,256]{2,1,0:T(8,128)(2,1)} %collective-permute-done.6), channel_id=1, source_target_pairs={{0,8},{8,16},{16,24},{1,9},{9,17},{17,25},{2,10},{10,18},{18,26},{... | collective-permute-start | bytes 1572872 | tf_op jit(solution)/shard_map/ppermute | solution.py:20
  463.0 1.9 constant_dynamic-update-slice_fusion.3
  464.9 1.9 constant_dynamic-update-slice_fusion.2
  467.6 2.0 constant_dynamic-update-slice_fusion
  473.5 5.6 fusion.81
  479.2 8.3 %fusion.70 = bf16[2,512,256]{2,1,0:T(8,128)(2,1)} fusion(bf16[2,2560,256]{2,1,0:T(8,128)(2,1)} %copy-done.17, f32[2,512]{1,0:T(2,128)S(1)} %fusion.81, f32[2,512,256]{2,1,0:T(8,128)S(1)} %copy-done.1, f32[256]{0:T(256)S(1)} %bitcast.95, f32[2,512]{1,0:T(2,128)S(1)} %add_rsqrt_fusion, f32[]{:T(128)} %bitcast.83, pred[512,2560]{1,0:T(8,128)(4,1)} %fusion.67, ...), kind=kOutput, calls=%fused_computation.84 | convolution fusion | flops 2698513920 | bytes 8659972 | tf_op jit(solution)/shard_map/sqk,skd->sqd/dot_general | solution.py:90
  487.7 85.2 %all_to_all.5 = bf16[8,1,256,512]{3,2,1,0:T(8,128)(2,1)S(1)} all-to-all(bf16[8,1,256,512]{3,2,1,0:T(8,128)(2,1)S(1)} %bitcast_dynamic-update-slice_fusion), channel_id=1, replica_groups=mesh['seq'=4,'head'=8] {'head'}, dimensions={0} | all-to-all | bytes 4194304 | tf_op jit(solution)/shard_map/all_to_all | solution.py:13
  574.2 5.5 convolution_convert_fusion
  (158 shorter events, 52.3 us)
Async XLA Ops:
  6.5 98.6 %copy-start = (bf16[4096,1]{0,1:T(2,128)(2,1)S(1)}, bf16[4096,1]{0,1:T(2,128)(2,1)}, u32[]{:S(2)}) copy-start(bf16[4096,1]{0,1:T(2,128)(2,1)} %param.14) | copy-start | bytes 24580
  6.5 87.2 %all-gather.3.cloned.1.call-start = ((), (), s32[]{:S(2)}) async-start(), calls=%async_computation.1 | async-start | bytes 9437184 | tf_op jit(solution)/shard_map/all_gather | solution.py:115
  7.3 566.9 %all-gather.5.cloned.1.call-start = ((), (), s32[]{:S(2)}) async-start(), calls=%async_computation.2 | async-start | bytes 4718592 | tf_op jit(solution)/shard_map/all_gather | solution.py:175
  93.7 11.4 %copy-start.6 = (bf16[1024,4096]{1,0:T(8,128)(2,1)S(1)}, bf16[1024,4096]{1,0:T(8,128)(2,1)}, u32[]{:S(2)}) copy-start(bf16[1024,4096]{1,0:T(8,128)(2,1)} %all-gather.3.cloned.1.call-done) | copy-start | bytes 25165828
  104.8 2.7 copy-start.7
  107.4 5.7 copy-start.2
  109.1 16.0 %collective-permute-start.2 = (bf16[2,512,256]{2,1,0:T(8,128)(2,1)}, bf16[2,512,256]{2,1,0:T(8,128)(2,1)S(1)}, u32[]{:S(2)}, u32[]{:S(2)}) collective-permute-start(bf16[2,512,256]{2,1,0:T(8,128)(2,1)} %bitcast.8), channel_id=1, source_target_pairs={{0,8},{8,16},{16,24},{1,9},{9,17},{17,25},{2,10},{10,18},{18,26},{... | collective-permute-start | bytes 1572872 | tf_op jit(solution)/shard_map/ppermute | solution.py:20
  118.0 0.8 copy-start.9
  118.8 17.4 %collective-permute-start.5 = (bf16[2,512,256]{2,1,0:T(8,128)(2,1)S(1)}, bf16[2,512,256]{2,1,0:T(8,128)(2,1)}, u32[]{:S(2)}, u32[]{:S(2)}) collective-permute-start(bf16[2,512,256]{2,1,0:T(8,128)(2,1)S(1)} %bitcast.88), channel_id=1, source_target_pairs={{0,8},{8,16},{16,24},{1,9},{9,17},{17,25},{2,10},{10,18},{18,26},{... | collective-permute-start | bytes 1572872 | tf_op jit(solution)/shard_map/ppermute | solution.py:20
  125.1 28.7 %copy-start.12 = (bf16[2,512,256]{2,1,0:T(8,128)(2,1)}, bf16[2,512,256]{2,1,0:T(8,128)(2,1)S(1)}, u32[]{:S(2)}) copy-start(bf16[2,512,256]{2,1,0:T(8,128)(2,1)S(1)} %collective-permute-done.2) | copy-start | bytes 1572868
  125.1 22.4 %collective-permute-start.3 = (bf16[2,512,256]{2,1,0:T(8,128)(2,1)S(1)}, bf16[2,512,256]{2,1,0:T(8,128)(2,1)}, u32[]{:S(2)}, u32[]{:S(2)}) collective-permute-start(bf16[2,512,256]{2,1,0:T(8,128)(2,1)S(1)} %collective-permute-done.2), channel_id=1, source_target_pairs={{0,8},{8,16},{16,24},{1,9},{9,17},{17,25},{2,10},{10,18},{18,26},{... | collective-permute-start | bytes 1572872 | tf_op jit(solution)/shard_map/ppermute | solution.py:20
  136.2 311.8 %collective-permute-start.6 = (bf16[2,512,256]{2,1,0:T(8,128)(2,1)}, bf16[2,512,256]{2,1,0:T(8,128)(2,1)}, u32[]{:S(2)}, u32[]{:S(2)}) collective-permute-start(bf16[2,512,256]{2,1,0:T(8,128)(2,1)} %collective-permute-done.5), channel_id=1, source_target_pairs={{0,8},{8,16},{16,24},{1,9},{9,17},{17,25},{2,10},{10,18},{18,26},{... | collective-permute-start | bytes 1572872 | tf_op jit(solution)/shard_map/ppermute | solution.py:20
  147.4 315.6 %collective-permute-start.4 = (bf16[2,512,256]{2,1,0:T(8,128)(2,1)}, bf16[2,512,256]{2,1,0:T(8,128)(2,1)}, u32[]{:S(2)}, u32[]{:S(2)}) collective-permute-start(bf16[2,512,256]{2,1,0:T(8,128)(2,1)} %collective-permute-done.3), channel_id=1, source_target_pairs={{0,8},{8,16},{16,24},{1,9},{9,17},{17,25},{2,10},{10,18},{18,26},{... | collective-permute-start | bytes 1572872 | tf_op jit(solution)/shard_map/ppermute | solution.py:20
  168.9 2.7 copy-start.3
  168.9 2.7 copy-start.14
  171.5 1.0 copy-start.4
  172.6 2.1 copy-start.5
  172.6 13.6 %collective-permute-start = (f32[256,512]{1,0:T(8,128)S(1)}, f32[256,512]{1,0:T(8,128)}, u32[]{:S(2)}, u32[]{:S(2)}) collective-permute-start(f32[256,512]{1,0:T(8,128)S(1)} %get-tuple-element.431), channel_id=1, source_target_pairs={{0,8},{8,16},{16,24},{1,9},{9,17},{17,25},{2,10},{10,18},{18,26},{... | collective-permute-start | bytes 1572872 | tf_op jit(solution)/shard_map/while/body/eval_jaxpr/ppermute | solution.py:20
  174.7 20.5 %collective-permute-start.1 = (f32[512,256]{1,0:T(8,128)}, f32[512,256]{1,0:T(8,128)S(1)}, u32[]{:S(2)}, u32[]{:S(2)}) collective-permute-start(f32[512,256]{1,0:T(8,128)} %copy-done.5), channel_id=1, source_target_pairs={{0,8},{8,16},{16,24},{1,9},{9,17},{17,25},{2,10},{10,18},{18,26},{... | collective-permute-start | bytes 1572872 | tf_op jit(solution)/shard_map/while/body/eval_jaxpr/ppermute | solution.py:20
  196.5 22.6 %copy-start.5 = (f32[512,256]{1,0:T(8,128)}, f32[512,256]{1,0:T(8,128)S(1)}, u32[]{:S(2)}) copy-start(f32[512,256]{1,0:T(8,128)S(1)} %get-tuple-element.432) | copy-start | bytes 1572868 | tf_op jit(solution)/shard_map/while
  196.5 34.1 %collective-permute-start = (f32[256,512]{1,0:T(8,128)S(1)}, f32[256,512]{1,0:T(8,128)}, u32[]{:S(2)}, u32[]{:S(2)}) collective-permute-start(f32[256,512]{1,0:T(8,128)S(1)} %get-tuple-element.431), channel_id=1, source_target_pairs={{0,8},{8,16},{16,24},{1,9},{9,17},{17,25},{2,10},{10,18},{18,26},{... | collective-permute-start | bytes 1572872 | tf_op jit(solution)/shard_map/while/body/eval_jaxpr/ppermute | solution.py:20
  219.1 19.6 %collective-permute-start.1 = (f32[512,256]{1,0:T(8,128)}, f32[512,256]{1,0:T(8,128)S(1)}, u32[]{:S(2)}, u32[]{:S(2)}) collective-permute-start(f32[512,256]{1,0:T(8,128)} %copy-done.5), channel_id=1, source_target_pairs={{0,8},{8,16},{16,24},{1,9},{9,17},{17,25},{2,10},{10,18},{18,26},{... | collective-permute-start | bytes 1572872 | tf_op jit(solution)/shard_map/while/body/eval_jaxpr/ppermute | solution.py:20
  240.0 5.1 copy-start.5
  240.0 26.8 %collective-permute-start = (f32[256,512]{1,0:T(8,128)S(1)}, f32[256,512]{1,0:T(8,128)}, u32[]{:S(2)}, u32[]{:S(2)}) collective-permute-start(f32[256,512]{1,0:T(8,128)S(1)} %get-tuple-element.431), channel_id=1, source_target_pairs={{0,8},{8,16},{16,24},{1,9},{9,17},{17,25},{2,10},{10,18},{18,26},{... | collective-permute-start | bytes 1572872 | tf_op jit(solution)/shard_map/while/body/eval_jaxpr/ppermute | solution.py:20
  245.1 28.3 %collective-permute-start.1 = (f32[512,256]{1,0:T(8,128)}, f32[512,256]{1,0:T(8,128)S(1)}, u32[]{:S(2)}, u32[]{:S(2)}) collective-permute-start(f32[512,256]{1,0:T(8,128)} %copy-done.5), channel_id=1, source_target_pairs={{0,8},{8,16},{16,24},{1,9},{9,17},{17,25},{2,10},{10,18},{18,26},{... | collective-permute-start | bytes 1572872 | tf_op jit(solution)/shard_map/while/body/eval_jaxpr/ppermute | solution.py:20
  274.8 12.1 %copy-start.5 = (f32[512,256]{1,0:T(8,128)}, f32[512,256]{1,0:T(8,128)S(1)}, u32[]{:S(2)}) copy-start(f32[512,256]{1,0:T(8,128)S(1)} %get-tuple-element.432) | copy-start | bytes 1572868 | tf_op jit(solution)/shard_map/while
  274.8 23.6 %collective-permute-start = (f32[256,512]{1,0:T(8,128)S(1)}, f32[256,512]{1,0:T(8,128)}, u32[]{:S(2)}, u32[]{:S(2)}) collective-permute-start(f32[256,512]{1,0:T(8,128)S(1)} %get-tuple-element.431), channel_id=1, source_target_pairs={{0,8},{8,16},{16,24},{1,9},{9,17},{17,25},{2,10},{10,18},{18,26},{... | collective-permute-start | bytes 1572872 | tf_op jit(solution)/shard_map/while/body/eval_jaxpr/ppermute | solution.py:20
  286.9 18.2 %collective-permute-start.1 = (f32[512,256]{1,0:T(8,128)}, f32[512,256]{1,0:T(8,128)S(1)}, u32[]{:S(2)}, u32[]{:S(2)}) collective-permute-start(f32[512,256]{1,0:T(8,128)} %copy-done.5), channel_id=1, source_target_pairs={{0,8},{8,16},{16,24},{1,9},{9,17},{17,25},{2,10},{10,18},{18,26},{... | collective-permute-start | bytes 1572872 | tf_op jit(solution)/shard_map/while/body/eval_jaxpr/ppermute | solution.py:20
  320.2 2.7 copy-start.3
  320.2 2.7 copy-start.14
  322.9 1.0 copy-start.4
  323.9 2.1 copy-start.5
  323.9 13.6 %collective-permute-start = (f32[256,512]{1,0:T(8,128)S(1)}, f32[256,512]{1,0:T(8,128)}, u32[]{:S(2)}, u32[]{:S(2)}) collective-permute-start(f32[256,512]{1,0:T(8,128)S(1)} %get-tuple-element.431), channel_id=1, source_target_pairs={{0,8},{8,16},{16,24},{1,9},{9,17},{17,25},{2,10},{10,18},{18,26},{... | collective-permute-start | bytes 1572872 | tf_op jit(solution)/shard_map/while/body/eval_jaxpr/ppermute | solution.py:20
  326.0 17.6 %collective-permute-start.1 = (f32[512,256]{1,0:T(8,128)}, f32[512,256]{1,0:T(8,128)S(1)}, u32[]{:S(2)}, u32[]{:S(2)}) collective-permute-start(f32[512,256]{1,0:T(8,128)} %copy-done.5), channel_id=1, source_target_pairs={{0,8},{8,16},{16,24},{1,9},{9,17},{17,25},{2,10},{10,18},{18,26},{... | collective-permute-start | bytes 1572872 | tf_op jit(solution)/shard_map/while/body/eval_jaxpr/ppermute | solution.py:20
  345.0 23.8 %copy-start.5 = (f32[512,256]{1,0:T(8,128)}, f32[512,256]{1,0:T(8,128)S(1)}, u32[]{:S(2)}) copy-start(f32[512,256]{1,0:T(8,128)S(1)} %get-tuple-element.432) | copy-start | bytes 1572868 | tf_op jit(solution)/shard_map/while
  345.0 34.8 %collective-permute-start = (f32[256,512]{1,0:T(8,128)S(1)}, f32[256,512]{1,0:T(8,128)}, u32[]{:S(2)}, u32[]{:S(2)}) collective-permute-start(f32[256,512]{1,0:T(8,128)S(1)} %get-tuple-element.431), channel_id=1, source_target_pairs={{0,8},{8,16},{16,24},{1,9},{9,17},{17,25},{2,10},{10,18},{18,26},{... | collective-permute-start | bytes 1572872 | tf_op jit(solution)/shard_map/while/body/eval_jaxpr/ppermute | solution.py:20
  368.7 16.8 %collective-permute-start.1 = (f32[512,256]{1,0:T(8,128)}, f32[512,256]{1,0:T(8,128)S(1)}, u32[]{:S(2)}, u32[]{:S(2)}) collective-permute-start(f32[512,256]{1,0:T(8,128)} %copy-done.5), channel_id=1, source_target_pairs={{0,8},{8,16},{16,24},{1,9},{9,17},{17,25},{2,10},{10,18},{18,26},{... | collective-permute-start | bytes 1572872 | tf_op jit(solution)/shard_map/while/body/eval_jaxpr/ppermute | solution.py:20
  386.8 5.1 copy-start.5
  386.8 26.8 %collective-permute-start = (f32[256,512]{1,0:T(8,128)S(1)}, f32[256,512]{1,0:T(8,128)}, u32[]{:S(2)}, u32[]{:S(2)}) collective-permute-start(f32[256,512]{1,0:T(8,128)S(1)} %get-tuple-element.431), channel_id=1, source_target_pairs={{0,8},{8,16},{16,24},{1,9},{9,17},{17,25},{2,10},{10,18},{18,26},{... | collective-permute-start | bytes 1572872 | tf_op jit(solution)/shard_map/while/body/eval_jaxpr/ppermute | solution.py:20
  392.0 26.8 %collective-permute-start.1 = (f32[512,256]{1,0:T(8,128)}, f32[512,256]{1,0:T(8,128)S(1)}, u32[]{:S(2)}, u32[]{:S(2)}) collective-permute-start(f32[512,256]{1,0:T(8,128)} %copy-done.5), channel_id=1, source_target_pairs={{0,8},{8,16},{16,24},{1,9},{9,17},{17,25},{2,10},{10,18},{18,26},{... | collective-permute-start | bytes 1572872 | tf_op jit(solution)/shard_map/while/body/eval_jaxpr/ppermute | solution.py:20
  420.0 10.9 %copy-start.5 = (f32[512,256]{1,0:T(8,128)}, f32[512,256]{1,0:T(8,128)S(1)}, u32[]{:S(2)}) copy-start(f32[512,256]{1,0:T(8,128)S(1)} %get-tuple-element.432) | copy-start | bytes 1572868 | tf_op jit(solution)/shard_map/while
  420.0 20.6 %collective-permute-start = (f32[256,512]{1,0:T(8,128)S(1)}, f32[256,512]{1,0:T(8,128)}, u32[]{:S(2)}, u32[]{:S(2)}) collective-permute-start(f32[256,512]{1,0:T(8,128)S(1)} %get-tuple-element.431), channel_id=1, source_target_pairs={{0,8},{8,16},{16,24},{1,9},{9,17},{17,25},{2,10},{10,18},{18,26},{... | collective-permute-start | bytes 1572872 | tf_op jit(solution)/shard_map/while/body/eval_jaxpr/ppermute | solution.py:20
  431.0 15.4 %collective-permute-start.1 = (f32[512,256]{1,0:T(8,128)}, f32[512,256]{1,0:T(8,128)S(1)}, u32[]{:S(2)}, u32[]{:S(2)}) collective-permute-start(f32[512,256]{1,0:T(8,128)} %copy-done.5), channel_id=1, source_target_pairs={{0,8},{8,16},{16,24},{1,9},{9,17},{17,25},{2,10},{10,18},{18,26},{... | collective-permute-start | bytes 1572872 | tf_op jit(solution)/shard_map/while/body/eval_jaxpr/ppermute | solution.py:20
  446.4 20.4 %copy-start.13 = (bf16[2,512,256]{2,1,0:T(8,128)(2,1)S(1)}, bf16[2,512,256]{2,1,0:T(8,128)(2,1)}, u32[]{:S(2)}) copy-start(bf16[2,512,256]{2,1,0:T(8,128)(2,1)} %copy-done.12) | copy-start | bytes 1572868
  446.4 23.3 %copy-start.16 = (bf16[2,2560,256]{2,1,0:T(8,128)(2,1)S(1)}, bf16[2,2560,256]{2,1,0:T(8,128)(2,1)}, u32[]{:S(2)}) copy-start(bf16[2,2560,256]{2,1,0:T(8,128)(2,1)} %broadcast_dynamic-update-slice_fusion) | copy-start | bytes 7864324
  448.0 21.7 %collective-permute-start.7 = (bf16[2,512,256]{2,1,0:T(8,128)(2,1)}, bf16[2,512,256]{2,1,0:T(8,128)(2,1)S(1)}, u32[]{:S(2)}, u32[]{:S(2)}) collective-permute-start(bf16[2,512,256]{2,1,0:T(8,128)(2,1)} %collective-permute-done.6), channel_id=1, source_target_pairs={{0,8},{8,16},{16,24},{1,9},{9,17},{17,25},{2,10},{10,18},{18,26},{... | collective-permute-start | bytes 1572872 | tf_op jit(solution)/shard_map/ppermute | solution.py:20
  466.8 5.2 copy-start.10
  467.6 5.9 %copy-start.11 = (pred[512,2560]{1,0:T(8,128)(4,1)S(1)}, pred[512,2560]{1,0:T(8,128)(4,1)}, u32[]{:S(2)}) copy-start(pred[512,2560]{1,0:T(8,128)(4,1)} %fusion.67) | copy-start | bytes 3932164
  467.6 5.9 %copy-start.15 = (bf16[2,512,256]{2,1,0:T(8,128)(2,1)S(1)}, bf16[2,512,256]{2,1,0:T(8,128)(2,1)}, u32[]{:S(2)}) copy-start(bf16[2,512,256]{2,1,0:T(8,128)(2,1)} %get-tuple-element.505) | copy-start | bytes 1572868
  472.0 1.5 copy-start.17
  473.5 5.6 copy-start.1
  473.5 5.7 copy-start.18
  479.2 8.3 %copy-start.8 = (bf16[1,256,4096]{2,1,0:T(8,128)(2,1)S(1)}, bf16[1,256,4096]{2,1,0:T(8,128)(2,1)}, u32[]{:S(2)}) copy-start(bf16[1,256,4096]{2,1,0:T(8,128)(2,1)} %param.19) | copy-start | bytes 6291460
Sparse Core Ops, SparseCore 0:
  8.9 84.7 all-gather.2
  487.6 86.5 all-gather.4
